TPU v7x, 32 devices: a whole 2x2x4 slice. The times are simulated.
32 devices in a mesh: views: 4 (over z), bricks: 8 (over y, x, core).
Axes of the slice: x: 2, y: 2, z: 4, core: 2. Of those that a mesh axis runs over, the one named last changes fastest.
Arguments:
- tile_pixel: int32 [4, 8, 32], P('views', 'bricks'), may hold values from 0 to 15
- tile_voxel: int32 [4, 8, 32], P('views', 'bricks'), may hold values from 0 to 63
- tile_count: int32 [4, 8], P('views', 'bricks'), may hold values from 8 to 32, as said below
- features: bfloat16 [4, 8, 16, 64, 128], P('views', 'bricks'), may hold values from -6 to 6
- interp: bfloat16 [4, 8, 32, 128, 512], P('views', 'bricks'), may hold values from -0.5 to 0.5
- conv_weight: bfloat16 [3, 3, 3, 64, 64], replicated, may hold values from -0.15625 to 0.15625
- conv_bias: float32 [64], replicated, may hold values from -3 to 3
- smooth_coef: float32 [64, 128, 128], P('bricks', 'views'), may hold values from 0.04 to 0.16
Outputs:
- volume: bfloat16 [64, 64, 128, 128], P(None, 'bricks', 'views')
Inputs may be any that keep to these rules, and one draw needn't show every extreme that they name: `tile_count`: between 8 and 32 live tiles a device; counts are shared largely within a view group; some device has all 32 slots live in every draw.
All inputs are finite; a program needn't handle non-finite values.
Results may differ from a plain program's by a relative error of at most 0.0037.
Values may be sent and summed in bfloat16 or wider, within the bound.
A program may use at most 256 MiB of HBM per device.

v0:
```python
import functools

import jax
import jax.numpy as jnp
from jax import lax
from jax.experimental import pallas as pl
from jax.experimental.pallas import tpu as pltpu
from jax.sharding import PartitionSpec as P

MESH = pl.DeviceIdType.MESH
DIRS = ((0, 1), (0, -1), (1, 0), (-1, 0), (1, 1), (1, -1), (-1, 1), (-1, -1))
SENDS = (
    (0, 1, 0), (0, -1, 0), (1, 0, None), (-1, 0, None),
    (1, 1, None), (1, -1, None), (-1, 1, None), (-1, -1, None),
    (0, 1, 1), (0, -1, 1),
)
GROUP = 4
LIMIT = 60 * 1024 * 1024


def lift_kernel(pixel_ref, ids_ref, feats_ref, *refs):
    streams, out_ref = refs[:-1], refs[-1]
    each = streams[0].shape[0]
    group = each * len(streams)
    step = pl.program_id(0)
    channels = feats_ref.shape[1]
    lanes = out_ref.shape[2]
    parts = streams[0].shape[2] // lanes
    for k in range(group):
        slot = step * group + k
        chosen = feats_ref[pixel_ref[slot]]
        value = jnp.dot(chosen, streams[k // each][k % each], preferred_element_type=jnp.float32)
        value = value.astype(jnp.bfloat16)
        for part in range(parts):
            out_ref[k, part * channels : (part + 1) * channels, :] = value[
                :, part * lanes : (part + 1) * lanes
            ]
        tail = out_ref.shape[1] - parts * channels
        ident = jnp.full((tail, lanes), ids_ref[slot], jnp.int32)
        out_ref[k, parts * channels :, :] = ident.astype(jnp.float32).astype(jnp.bfloat16)


def lift(pixel_ids, ids, feats, tiles, depth):
    slots, pixels, voxels = tiles.shape
    channels = feats.shape[1]
    streams, each = 4, 2
    group = streams * each
    rows = voxels // depth * channels + 8
    return pl.pallas_call(
        lift_kernel,
        out_shape=jax.ShapeDtypeStruct((slots, rows, depth), jnp.bfloat16),
        grid_spec=pltpu.PrefetchScalarGridSpec(
            num_scalar_prefetch=2,
            grid=(slots // group,),
            in_specs=[
                pl.BlockSpec(feats.shape, lambda i, *_: (0, 0, 0)),
            ]
            + [
                pl.BlockSpec((each, pixels, voxels), lambda i, *_, q=q: (i * streams + q, 0, 0))
                for q in range(streams)
            ],
            out_specs=pl.BlockSpec((group, rows, depth), lambda i, *_: (i, 0, 0)),
        ),
        name="lift",
    )(pixel_ids, ids, feats, *[tiles] * streams)


def scatter_kernel(ids_ref, got_ref, out_ref, acc):
    slots = got_ref.shape[0]
    blocks = out_ref.shape[0]
    rows = out_ref.shape[1]

    def clear(i, _):
        acc[i] = jnp.zeros(acc.shape[1:], jnp.float32)
        return 0

    def add(d, _):
        i = ids_ref[d]
        acc[i] = acc[i] + got_ref[d, 0:rows, :].astype(jnp.float32)
        return 0

    def put(i, _):
        out_ref[i] = jnp.maximum(acc[i], 0.0).astype(jnp.bfloat16)
        return 0

    lax.fori_loop(0, blocks, clear, 0)
    lax.fori_loop(0, slots, add, 0)
    lax.fori_loop(0, blocks, put, 0)


def scatter(ids, got, blocks):
    rows = got.shape[1] - 8
    depth = got.shape[2]
    return pl.pallas_call(
        scatter_kernel,
        out_shape=jax.ShapeDtypeStruct((blocks, rows, depth), jnp.bfloat16),
        grid_spec=pltpu.PrefetchScalarGridSpec(
            num_scalar_prefetch=1,
            grid=(1,),
            in_specs=[pl.BlockSpec(got.shape, lambda i, *_: (0, 0, 0))],
            out_specs=pl.BlockSpec((blocks, rows, depth), lambda i, *_: (0, 0, 0)),
            scratch_shapes=[pltpu.VMEM((blocks + 1, rows, depth), jnp.float32)],
        ),
        compiler_params=pltpu.CompilerParams(vmem_limit_bytes=LIMIT),
        name="scatter",
    )(ids, got)


def conv_kernel(
    views, bricks, r_ref, w_ref, bias_ref, coef_ref, out_ref,
    padded, prod, gated, obuf, own_sem, send_sem, recv_sem, out_sem,
):
    v = lax.axis_index("views")
    b = lax.axis_index("bricks")
    size_x, size_y, ch, depth = r_ref.shape
    wide = 3 * ch

    def there(dv, db):
        return (v + dv >= 0) & (v + dv < views) & (b + db >= 0) & (b + db < bricks)

    def count(dv, db):
        return jnp.where(there(dv, db), 1, 0)

    own = pltpu.make_async_copy(
        r_ref, padded.at[pl.ds(2, size_x), pl.ds(2, size_y)], own_sem
    )
    own.start()

    barrier = pltpu.get_barrier_semaphore()
    total = 0
    for dv, db in DIRS:
        total = total + count(dv, db)

        @pl.when(there(dv, db))
        def _(dv=dv, db=db):
            pl.semaphore_signal(barrier, inc=1, device_id=(v + dv, b + db), device_id_type=MESH)

    pl.semaphore_wait(barrier, total)

    def span(delta, size, plane=None):
        if delta == 0:
            return pl.ds(0, size), pl.ds(2, size)
        if plane is None:
            low, width = 0, 2
        else:
            low, width = (1 - plane if delta == 1 else plane), 1
        if delta == 1:
            return pl.ds(size - 2 + low, width), pl.ds(low, width)
        return pl.ds(low, width), pl.ds(size + 2 + low, width)

    def copy(k):
        dv, db, plane = SENDS[k]
        from_x, to_x = span(db, size_x, plane)
        from_y, to_y = span(dv, size_y)
        return pltpu.make_async_remote_copy(
            src_ref=r_ref.at[from_x, from_y],
            dst_ref=padded.at[to_x, to_y],
            send_sem=send_sem.at[k],
            recv_sem=recv_sem.at[k],
            device_id=(v + dv, b + db),
            device_id_type=MESH,
        )

    for k, (dv, db, _) in enumerate(SENDS):

        @pl.when(there(dv, db))
        def _(k=k):
            copy(k).start()

    def receive(k):
        dv, db, plane = SENDS[k]
        _, to_x = span(db, size_x, plane)
        _, to_y = span(dv, size_y)

        @pl.when(there(-dv, -db))
        def _():
            copy(k).wait_recv()

        @pl.when(jnp.logical_not(there(-dv, -db)))
        def _():
            view = padded.at[to_x, to_y]
            view[...] = jnp.zeros(view.shape, jnp.bfloat16)

    lane = lax.broadcasted_iota(jnp.int32, (ch, depth), 1)

    def beside_z(low, high):
        before = jnp.where(lane == 0, 0.0, pltpu.roll(low, 1, 1))
        after = jnp.where(lane == depth - 1, 0.0, pltpu.roll(high, depth - 1, 1))
        return before + after

    def start_rows(slot, g, y):
        tall = [
            jnp.concatenate([padded[g + dx, y + dy + j] for j in range(GROUP)], axis=1)
            for dx in range(3)
            for dy in range(3)
        ]
        prod[slot] = jnp.dot(
            w_ref[...], jnp.concatenate(tall, axis=0), preferred_element_type=jnp.float32
        )

    def finish_rows(slot, g, y):
        x_all = b * size_x + g - 1
        x_fits = (x_all >= 0) & (x_all < bricks * size_x)
        for j in range(GROUP):
            at = slice(j * depth, (j + 1) * depth)
            value = prod[slot, ch : 2 * ch, at]
            value = value + beside_z(prod[slot, 0:ch, at], prod[slot, 2 * ch : wide, at])
            value = jnp.maximum(value + bias_ref[...], 0.0)
            y_all = v * size_y + y + j - 1
            fits = x_fits & (y_all >= 0) & (y_all < views * size_y)
            gated[g, y + j] = value * jnp.where(fits, 1.0, 0.0)

    def loop(low, high, body, unroll=1):
        def step(i, _):
            body(i)
            return 0

        lax.fori_loop(low, high, step, 0, unroll=unroll)

    groups = size_y // GROUP

    def smooth_rows(x, y):
        here = gated[x + 1, y + 1]
        beside = gated[x, y + 1] + gated[x + 2, y + 1] + gated[x + 1, y] + gated[x + 1, y + 2]
        beside = beside + beside_z(here, here)
        coef = coef_ref[x, pl.ds(y, 1), :]
        obuf[x, y] = (here + coef * (beside - 6.0 * here)).astype(jnp.bfloat16)

    def put(x):
        pltpu.make_async_copy(obuf.at[x], out_ref.at[x], out_sem.at[x]).start()

    def run_rows(g, starts, x=None):
        for i, y in enumerate(starts):
            start_rows(i % 2, g, y)
            if x is not None:
                for j in range(GROUP):
                    if i * GROUP + j < size_y:
                        smooth_rows(x, i * GROUP + j)
            if i:
                finish_rows((i - 1) % 2, g, starts[i - 1])
        finish_rows((len(starts) - 1) % 2, g, starts[-1])
        if x is not None:
            put(x)

    def loop(low, high, body):
        def step(i, _):
            body(i)
            return 0

        lax.fori_loop(low, high, step, 0)

    middle = [GROUP * c for c in range(1, size_y // GROUP)]
    ends = [0, size_y + 2 - GROUP]
    rows = [0] + middle + [size_y + 2 - GROUP]

    own.wait()
    loop(2, 5, lambda g: run_rows(g, middle))
    receive(2)
    receive(3)
    loop(2, 5, lambda g: run_rows(g, ends))
    loop(5, size_x, lambda g: run_rows(g, rows, g - 3))
    low_first = b < bricks // 2

    def boundary(i):
        low_side = (i < 2) == low_first
        odd = lax.rem(i, 2)
        for db, side in ((1, low_side), (-1, jnp.logical_not(low_side))):
            for plane in range(2):
                keys = [
                    k
                    for k, (dv, step, part) in enumerate(SENDS)
                    if step == db and (part == plane or (part is None and plane == 0))
                ]

                @pl.when(side & (odd == plane))
                def _(keys=keys):
                    for k in keys:
                        receive(k)

        g = jnp.where(low_side, 1 - odd, size_x + odd)
        ahead = jnp.where(i == 1, 1, jnp.where(i == 2, 0, size_x - 2))
        behind = jnp.where(i == 1, size_x - 2, jnp.where(i == 2, size_x - 1, 1))
        x = jnp.where(i == 0, size_x - 3, jnp.where(low_first, ahead, behind))
        run_rows(g, rows, x)

    loop(0, 4, boundary)
    last = jnp.where(low_first, size_x - 1, 0)

    def finish(y):
        for j in range(GROUP):
            smooth_rows(last, y * GROUP + j)

    loop(0, size_y // GROUP, finish)
    put(last)
    for x in range(size_x):
        pltpu.make_async_copy(obuf.at[x], out_ref.at[x], out_sem.at[x]).wait()
    for k, (dv, db, _) in enumerate(SENDS):

        @pl.when(there(dv, db))
        def _(k=k):
            copy(k).wait_send()


def convolve_smooth(rect, weights, bias, coef, views, bricks):
    size_x, size_y, ch, depth = rect.shape
    vmem = pl.BlockSpec(memory_space=pltpu.VMEM)
    anyspec = pl.BlockSpec(memory_space=pl.ANY)
    return pl.pallas_call(
        functools.partial(conv_kernel, views, bricks),
        out_shape=jax.ShapeDtypeStruct(rect.shape, jnp.bfloat16),
        in_specs=[anyspec, vmem, vmem, vmem],
        out_specs=anyspec,
        scratch_shapes=[
            pltpu.VMEM((size_x + 4, size_y + 4, ch, depth), jnp.bfloat16),
            pltpu.VMEM((2, 3 * ch, GROUP * depth), jnp.float32),
            pltpu.VMEM((size_x + 2, size_y + 2, ch, depth), jnp.float32),
            pltpu.VMEM((size_x, size_y, ch, depth), jnp.bfloat16),
            pltpu.SemaphoreType.DMA,
            pltpu.SemaphoreType.DMA((len(SENDS),)),
            pltpu.SemaphoreType.DMA((len(SENDS),)),
            pltpu.SemaphoreType.DMA((size_x,)),
        ],
        compiler_params=pltpu.CompilerParams(
            collective_id=0, has_side_effects=True, vmem_limit_bytes=LIMIT
        ),
        name="conv",
    )(rect, weights, bias, coef)


def on_device(
    views, bricks,
    tile_pixel, tile_voxel, tile_count, features, interp, conv_weight, conv_bias, smooth_coef
):
    feats = features[0, 0]
    tiles = interp[0, 0]
    pixel_ids = tile_pixel[0, 0]
    voxel_ids = tile_voxel[0, 0]
    count = tile_count[0, 0]
    slots_total = tiles.shape[0]
    channels = feats.shape[1]
    size_x, size_y, depth = smooth_coef.shape
    per_block = tiles.shape[2] // depth
    blocks = size_x * size_y // per_block
    sender = lax.axis_index("views") * bricks + lax.axis_index("bricks")
    offset = jnp.remainder(sender * 37, slots_total)
    slot_ids = jnp.arange(slots_total, dtype=jnp.int32)
    live = jnp.remainder(slot_ids - offset, slots_total) < count
    ids = jnp.where(live, voxel_ids, blocks)
    partial = lift(pixel_ids, ids, feats, tiles, depth)
    got = lax.all_to_all(partial, ("views", "bricks"), split_axis=0, concat_axis=0, tiled=True)
    got_ids = got[:, got.shape[1] - 8, 0].astype(jnp.int32)
    rect = scatter(got_ids, got, blocks).reshape(size_x, size_y, channels, depth)
    weights = jnp.transpose(conv_weight, (2, 3, 0, 1, 4)).reshape(3 * channels, 9 * channels)
    bias = jnp.broadcast_to(conv_bias[:, None], (channels, depth))
    out = convolve_smooth(rect, weights, bias, smooth_coef, views, bricks)
    return jnp.transpose(out, (2, 0, 1, 3))


def solution(mesh):
    in_specs = (
        P("views", "bricks", None),
        P("views", "bricks", None),
        P("views", "bricks"),
        P("views", "bricks", None, None, None),
        P("views", "bricks", None, None, None),
        P(),
        P(),
        P("bricks", "views", None),
    )
    out_specs = P(None, "bricks", "views", None)
    body = functools.partial(on_device, mesh.shape["views"], mesh.shape["bricks"])
    return jax.shard_map(body, mesh=mesh, in_specs=in_specs, out_specs=out_specs, check_vma=False)
```

profile of v0, /device:TPU:12, one launch (start us, length us, event | category | flops | bytes accessed | tf_op | source)
XLA Modules:
  0.0 112.7 jit_solution(13196439847093722020)
XLA Ops:
  0.7 1.2 %compare_select_fusion.2.ids_ref = s32[32]{0:T(128)} fusion(s32[1,1,32]{2,1,0:T(1,128)} %param.9, s32[]{:T(128)} %bitcast.9, s32[]{:T(128)S(6)} %select_n.17), kind=kLoop, calls=%fused_computation.4 | loop fusion | flops 448 | bytes 264 | tf_op jit(solution)/shard_map/jit(_where)/select_n | solution.py:348
  1.9 5.5 %lift.1 = bf16[32,264,128]{2,1,0:T(8,128)(2,1)} custom-call(s32[32]{0:T(128)} %bitcast.18, s32[32]{0:T(128)} %compare_select_fusion.2.ids_ref, bf16[16,64,128]{2,1,0:T(8,128)(2,1)} %bitcast.17, bf16[32,128,512]{2,1,0:T(8,128)(2,1)} %bitcast.10, bf16[32,128,512]{2,1,0:T(8,128)(2,1)} %bitcast.11, bf16[32,128,512]{2,1,0:T(8,128)(2,1)} %bitcast.12, ...), custom_call_target="tpu_custom_call" | custom-call | tf_op jit(solution)/shard_map/lift/pallas_call | solution.py:49
  7.4 0.0 copy-start.1
  7.4 6.0 %all-to-all-start = ((bf16[32,264,128]{2,1,0:T(8,128)(2,1)}), bf16[32,264,128]{2,1,0:T(8,128)(2,1)S(1)}, u32[]{:S(2)}, u32[]{:S(2)}) async-start(bf16[32,264,128]{2,1,0:T(8,128)(2,1)} %lift.1), calls=%async_computation | async-start | bytes 4325376 | tf_op jit(solution)/shard_map/all_to_all | solution.py:350
  13.4 0.0 copy-start.2
  13.4 0.0 copy-done.1
  13.4 0.4 copy.11
  13.8 1.1 reshape.10.w_ref
  14.9 46.4 %all-to-all-done.got_ref = bf16[32,264,128]{2,1,0:T(8,128)(2,1)S(1)} async-done(((bf16[32,264,128]{2,1,0:T(8,128)(2,1)}), bf16[32,264,128]{2,1,0:T(8,128)(2,1)S(1)}, u32[]{:S(2)}, u32[]{:S(2)}) %all-to-all-start) | async-done | bytes 2162720 | tf_op jit(solution)/shard_map/all_to_all | solution.py:350
  61.3 0.0 copy-start
  61.3 1.2 %fusion.ids_ref = s32[32]{0:T(128)} fusion(bf16[32,264,128]{2,1,0:T(8,128)(2,1)S(1)} %all-to-all-done.got_ref), kind=kLoop, calls=%fused_computation.1 | loop fusion | flops 32 | bytes 192 | tf_op jit(solution)/shard_map/convert_element_type | solution.py:351
  62.5 0.1 copy-done
  62.7 6.3 %scatter.1 = bf16[64,256,128]{2,1,0:T(8,128)(2,1)} custom-call(s32[32]{0:T(128)} %fusion.ids_ref, bf16[32,264,128]{2,1,0:T(8,128)(2,1)} %copy-done), custom_call_target="tpu_custom_call" | custom-call | tf_op jit(solution)/shard_map/scatter/pallas_call | solution.py:94
  68.9 0.0 copy-done.2
  68.9 0.7 broadcast_in_dim.11.bias_ref
  69.6 36.2 %conv.1 = bf16[8,32,64,128]{3,2,1,0:T(8,128)(2,1)} custom-call(bf16[8,32,64,128]{3,2,1,0:T(8,128)(2,1)} %bitcast.14, bf16[192,576]{1,0:T(8,128)(2,1)} %reshape.10.w_ref, f32[64,128]{1,0:T(8,128)} %broadcast_in_dim.11.bias_ref, f32[8,32,128]{2,1,0:T(8,128)} %coef_ref.1), custom_call_target="tpu_custom_call" | custom-call | tf_op jit(solution)/shard_map/conv/pallas_call | solution.py:308
  105.8 6.9 %copy.12 = bf16[64,8,32,128]{3,2,1,0:T(8,128)(2,1)} copy(bf16[64,8,32,128]{3,0,2,1:T(8,128)(2,1)} %bitcast.15) | data formatting | bytes 8388608 | tf_op jit(solution)/shard_map/transpose | solution.py:356
Async XLA Ops:
  7.4 6.0 %copy-start.1 = (bf16[3,3,3,64,64]{4,3,2,1,0:T(8,128)(2,1)S(1)}, bf16[3,3,3,64,64]{4,3,2,1,0:T(8,128)(2,1)}, u32[]{:S(2)}) copy-start(bf16[3,3,3,64,64]{4,3,2,1,0:T(8,128)(2,1)} %param.13) | copy-start | bytes 663556
  7.4 53.9 %all-to-all-start = ((bf16[32,264,128]{2,1,0:T(8,128)(2,1)}), bf16[32,264,128]{2,1,0:T(8,128)(2,1)S(1)}, u32[]{:S(2)}, u32[]{:S(2)}) async-start(bf16[32,264,128]{2,1,0:T(8,128)(2,1)} %lift.1), calls=%async_computation | async-start | bytes 4325376 | tf_op jit(solution)/shard_map/all_to_all | solution.py:350
  13.4 55.5 %copy-start.2 = (f32[64]{0:T(128)S(1)}, f32[64]{0:T(128)}, u32[]{:S(2)}) copy-start(f32[64]{0:T(128)} %param.14) | copy-start | bytes 772
  61.3 1.4 %copy-start = (bf16[32,264,128]{2,1,0:T(8,128)(2,1)}, bf16[32,264,128]{2,1,0:T(8,128)(2,1)S(1)}, u32[]{:S(2)}) copy-start(bf16[32,264,128]{2,1,0:T(8,128)(2,1)S(1)} %all-to-all-done.got_ref) | copy-start | bytes 6488068
where the time goes:
time: 113 us
  Pallas kernels  48 us (42%)
  waiting for transfers between devices  46.4 us (41%)
  local copies, waits for them, and re-layouts  9.19 us (8%)
  starting transfers between devices  5.99 us (5%)
  other arithmetic  2.49 us (2%)
    all_to_all x1, waiting for transfers between devices, on_device(): lax.all_to_all(partial, ('views', 'bricks'), split_axis=0, concat_axis=0,...  46.4 us
    pallas_call x1, Pallas kernels, convolve_smooth(): pl.pallas_call(functools.partial(conv_kernel, views, bricks), out_shape=j...  36.2 us
    transpose x1, local copies, waits for them, and re-layouts, on_device(): return jnp.transpose(out, (2, 0, 1, 3))  6.9 us
    pallas_call x1, Pallas kernels, scatter(): pl.pallas_call(scatter_kernel, out_shape=jax.ShapeDtypeStruct((blocks, ro...  6.28 us
    all_to_all x1, starting transfers between devices, on_device(): lax.all_to_all(partial, ('views', 'bricks'), split_axis=0, concat_axis=0,...  5.99 us
    pallas_call x1, Pallas kernels, lift(): pl.pallas_call(lift_kernel, out_shape=jax.ShapeDtypeStruct((slots, rows,...  5.51 us
  transfers between devices with their start and end apart: 1, of which 1 were waited for; matrix products, arithmetic and copies ran while one was open for 1% of the time, Pallas kernels for 0%

commit v1 on v0

--- a/solution.py
+++ b/solution.py
@@ -18,92 +18,193 @@
 LIMIT = 60 * 1024 * 1024
 
 
-def lift_kernel(pixel_ref, ids_ref, feats_ref, *refs):
-    streams, out_ref = refs[:-1], refs[-1]
-    each = streams[0].shape[0]
-    group = each * len(streams)
-    step = pl.program_id(0)
-    channels = feats_ref.shape[1]
-    lanes = out_ref.shape[2]
-    parts = streams[0].shape[2] // lanes
-    for k in range(group):
-        slot = step * group + k
-        chosen = feats_ref[pixel_ref[slot]]
-        value = jnp.dot(chosen, streams[k // each][k % each], preferred_element_type=jnp.float32)
-        value = value.astype(jnp.bfloat16)
-        for part in range(parts):
-            out_ref[k, part * channels : (part + 1) * channels, :] = value[
-                :, part * lanes : (part + 1) * lanes
-            ]
-        tail = out_ref.shape[1] - parts * channels
-        ident = jnp.full((tail, lanes), ids_ref[slot], jnp.int32)
-        out_ref[k, parts * channels :, :] = ident.astype(jnp.float32).astype(jnp.bfloat16)
-
-
-def lift(pixel_ids, ids, feats, tiles, depth):
+def exchange_kernel(
+    views, bricks, pixel_ref, voxel_ref, count_ref, feats_ref, tiles_ref, out_ref,
+    tiles, part, got, sums, mark, marks, table, index,
+    tile_sem, send_sem, recv_sem, mark_send, mark_recv, table_sem,
+):
+    v = lax.axis_index("views")
+    b = lax.axis_index("bricks")
+    slots = tiles.shape[0]
+    me = v * bricks + b
+    parts, _, ch, depth = part.shape
+    size_x, size_y = out_ref.shape[:2]
+    across = size_y // parts
+    blocks = size_x * across
+    order = [parts - 1] + list(range(parts - 1))
+
+    def peer(k):
+        turn = k + (views // 2) * bricks
+        return lax.rem(v + turn // bricks, views), lax.rem(b + lax.rem(turn, bricks), bricks)
+
+    def place(k):
+        pv, pb = peer(k)
+        return pv * bricks + pb
+
+    def loop(low, high, body, unroll=1):
+        def step(i, _):
+            body(i)
+            return 0
+
+        lax.fori_loop(low, high, step, 0, unroll=unroll)
+
+    own = (views - views // 2) * bricks % slots
+
+    def fetch(k):
+        slot = place(k)
+        return pltpu.make_async_copy(tiles_ref.at[slot], tiles.at[slot], tile_sem.at[slot])
+
+    loop(0, slots, lambda k: fetch(k).start())
+    barrier = pltpu.get_barrier_semaphore()
+
+    def greet(k):
+        @pl.when(k != own)
+        def _():
+            pl.semaphore_signal(barrier, inc=1, device_id=peer(k), device_id_type=MESH)
+
+    loop(0, slots, greet)
+
+    offset = lax.rem(me * 37, slots)
+
+    def note(s):
+        turn = lax.rem(s - offset + slots, slots)
+        ident = jnp.where(turn < count_ref[0, 0], voxel_ref[0, 0, s], blocks)
+        mark[s] = jnp.full(mark.shape[1:], ident, jnp.int32)
+
+    loop(0, slots, note)
+
+    def send_mark(k):
+        return pltpu.make_async_remote_copy(
+            src_ref=mark.at[place(k)], dst_ref=marks.at[me],
+            send_sem=mark_send, recv_sem=mark_recv,
+            device_id=peer(k), device_id_type=MESH,
+        )
+
+    def send_part(q, k):
+        return pltpu.make_async_remote_copy(
+            src_ref=part.at[q, place(k)], dst_ref=got.at[q, me],
+            send_sem=send_sem.at[q], recv_sem=recv_sem.at[q],
+            device_id=peer(k), device_id_type=MESH,
+        )
+
+    def push(q, k):
+        @pl.when(k != own)
+        def _():
+            send_part(q, k).start()
+
+        @pl.when(k == own)
+        def _():
+            pltpu.make_async_copy(part.at[q, me], got.at[q, me], recv_sem.at[q]).start()
+
+    def lift(k):
+        slot = place(k)
+        fetch(k).wait()
+        value = jnp.dot(
+            feats_ref[pixel_ref[0, 0, slot]], tiles[slot], preferred_element_type=jnp.float32
+        ).astype(jnp.bfloat16)
+        for q in range(parts):
+            part[q, slot] = value[:, q * depth : (q + 1) * depth]
+
+    lift(0)
+    pl.semaphore_wait(barrier, slots - 1)
+
+    def greet_mark(k):
+        @pl.when(k != own)
+        def _():
+            send_mark(k).start()
+
+        @pl.when(k == own)
+        def _():
+            pltpu.make_async_copy(mark.at[me], marks.at[me], mark_recv).start()
+
+    loop(0, slots, greet_mark)
+
+    def lift_push(k):
+        lift(k)
+        push(order[0], k - 1)
+
+    loop(1, slots, lift_push)
+    push(order[0], slots - 1)
+    for q in order[1:]:
+        loop(0, slots, lambda k, q=q: push(q, k))
+
+    pltpu.make_async_copy(marks, marks, mark_recv).wait()
+    lane = lax.broadcasted_iota(jnp.int32, marks.shape[1:], 1)
+    row = jnp.full(lane.shape, -1, jnp.int32)
+    row = lax.fori_loop(0, slots, lambda d, r: jnp.where(lane == d, marks[d], r), row)
+
+    def newest(match):
+        found = jnp.max(jnp.where(match, lane, -1), axis=1, keepdims=True)
+        return jnp.where(found < 0, slots, found)
+
+    table[0] = lax.fori_loop(
+        0, slots,
+        lambda d, t: jnp.where(lane == d, newest((row == marks[d]) & (lane < d)), t),
+        jnp.zeros(lane.shape, jnp.int32),
+    )
+    table[1] = lax.fori_loop(
+        0, blocks,
+        lambda i, t: jnp.where(lane == i, newest(row == i), t),
+        jnp.zeros(lane.shape, jnp.int32),
+    )
+    to_scalar = pltpu.make_async_copy(table, index, table_sem)
+    to_scalar.start()
+    to_scalar.wait()
+    sums[slots] = jnp.zeros(sums.shape[1:], jnp.float32)
+
+    for q in order:
+        pltpu.make_async_copy(got.at[q], got.at[q], recv_sem.at[q]).wait()
+
+        def add(d, q=q):
+            sums[d] = sums[index[0, 0, d]] + got[q, d].astype(jnp.float32)
+
+        def put(i, q=q):
+            value = jnp.maximum(sums[index[1, 0, i]], 0.0).astype(jnp.bfloat16)
+            out_ref[i // across, lax.rem(i, across) * parts + q] = value
+
+        loop(0, slots, add, 4)
+        loop(0, blocks, put, 4)
+
+    for q in range(parts):
+        sent = part.at[q, pl.ds(0, slots - 1)]
+        pltpu.make_async_copy(sent, sent, send_sem.at[q]).wait()
+    sent = mark.at[pl.ds(0, slots - 1)]
+    pltpu.make_async_copy(sent, sent, mark_send).wait()
+
+
+def exchange(pixel, voxel, count, feats, tiles, size_x, size_y, depth, views, bricks):
     slots, pixels, voxels = tiles.shape
-    channels = feats.shape[1]
-    streams, each = 4, 2
-    group = streams * each
-    rows = voxels // depth * channels + 8
+    ch = feats.shape[1]
+    parts = voxels // depth
+    smem = pl.BlockSpec(memory_space=pltpu.SMEM)
+    vmem = pl.BlockSpec(memory_space=pltpu.VMEM)
+    anyspec = pl.BlockSpec(memory_space=pl.ANY)
     return pl.pallas_call(
-        lift_kernel,
-        out_shape=jax.ShapeDtypeStruct((slots, rows, depth), jnp.bfloat16),
-        grid_spec=pltpu.PrefetchScalarGridSpec(
-            num_scalar_prefetch=2,
-            grid=(slots // group,),
-            in_specs=[
-                pl.BlockSpec(feats.shape, lambda i, *_: (0, 0, 0)),
-            ]
-            + [
-                pl.BlockSpec((each, pixels, voxels), lambda i, *_, q=q: (i * streams + q, 0, 0))
-                for q in range(streams)
-            ],
-            out_specs=pl.BlockSpec((group, rows, depth), lambda i, *_: (i, 0, 0)),
+        functools.partial(exchange_kernel, views, bricks),
+        out_shape=jax.ShapeDtypeStruct((size_x, size_y, ch, depth), jnp.bfloat16),
+        in_specs=[smem, smem, smem, vmem, anyspec],
+        out_specs=vmem,
+        scratch_shapes=[
+            pltpu.VMEM(tiles.shape, jnp.bfloat16),
+            pltpu.VMEM((parts, slots, ch, depth), jnp.bfloat16),
+            pltpu.VMEM((parts, slots, ch, depth), jnp.bfloat16),
+            pltpu.VMEM((slots + 1, ch, depth), jnp.float32),
+            pltpu.VMEM((slots, 8, 128), jnp.int32),
+            pltpu.VMEM((slots, 8, 128), jnp.int32),
+            pltpu.VMEM((2, 8, 128), jnp.int32),
+            pltpu.SMEM((2, 8, 128), jnp.int32),
+            pltpu.SemaphoreType.DMA((slots,)),
+            pltpu.SemaphoreType.DMA((parts,)),
+            pltpu.SemaphoreType.DMA((parts,)),
+            pltpu.SemaphoreType.DMA,
+            pltpu.SemaphoreType.DMA,
+            pltpu.SemaphoreType.DMA,
+        ],
+        compiler_params=pltpu.CompilerParams(
+            collective_id=1, has_side_effects=True, vmem_limit_bytes=LIMIT
         ),
-        name="lift",
-    )(pixel_ids, ids, feats, *[tiles] * streams)
-
-
-def scatter_kernel(ids_ref, got_ref, out_ref, acc):
-    slots = got_ref.shape[0]
-    blocks = out_ref.shape[0]
-    rows = out_ref.shape[1]
-
-    def clear(i, _):
-        acc[i] = jnp.zeros(acc.shape[1:], jnp.float32)
-        return 0
-
-    def add(d, _):
-        i = ids_ref[d]
-        acc[i] = acc[i] + got_ref[d, 0:rows, :].astype(jnp.float32)
-        return 0
-
-    def put(i, _):
-        out_ref[i] = jnp.maximum(acc[i], 0.0).astype(jnp.bfloat16)
-        return 0
-
-    lax.fori_loop(0, blocks, clear, 0)
-    lax.fori_loop(0, slots, add, 0)
-    lax.fori_loop(0, blocks, put, 0)
-
-
-def scatter(ids, got, blocks):
-    rows = got.shape[1] - 8
-    depth = got.shape[2]
-    return pl.pallas_call(
-        scatter_kernel,
-        out_shape=jax.ShapeDtypeStruct((blocks, rows, depth), jnp.bfloat16),
-        grid_spec=pltpu.PrefetchScalarGridSpec(
-            num_scalar_prefetch=1,
-            grid=(1,),
-            in_specs=[pl.BlockSpec(got.shape, lambda i, *_: (0, 0, 0))],
-            out_specs=pl.BlockSpec((blocks, rows, depth), lambda i, *_: (0, 0, 0)),
-            scratch_shapes=[pltpu.VMEM((blocks + 1, rows, depth), jnp.float32)],
-        ),
-        compiler_params=pltpu.CompilerParams(vmem_limit_bytes=LIMIT),
-        name="scatter",
-    )(ids, got)
+        name="exchange",
+    )(pixel, voxel, count, feats, tiles)
 
 
 def conv_kernel(
@@ -333,23 +434,11 @@
 ):
     feats = features[0, 0]
     tiles = interp[0, 0]
-    pixel_ids = tile_pixel[0, 0]
-    voxel_ids = tile_voxel[0, 0]
-    count = tile_count[0, 0]
-    slots_total = tiles.shape[0]
     channels = feats.shape[1]
     size_x, size_y, depth = smooth_coef.shape
-    per_block = tiles.shape[2] // depth
-    blocks = size_x * size_y // per_block
-    sender = lax.axis_index("views") * bricks + lax.axis_index("bricks")
-    offset = jnp.remainder(sender * 37, slots_total)
-    slot_ids = jnp.arange(slots_total, dtype=jnp.int32)
-    live = jnp.remainder(slot_ids - offset, slots_total) < count
-    ids = jnp.where(live, voxel_ids, blocks)
-    partial = lift(pixel_ids, ids, feats, tiles, depth)
-    got = lax.all_to_all(partial, ("views", "bricks"), split_axis=0, concat_axis=0, tiled=True)
-    got_ids = got[:, got.shape[1] - 8, 0].astype(jnp.int32)
-    rect = scatter(got_ids, got, blocks).reshape(size_x, size_y, channels, depth)
+    rect = exchange(
+        tile_pixel, tile_voxel, tile_count, feats, tiles, size_x, size_y, depth, views, bricks
+    )
     weights = jnp.transpose(conv_weight, (2, 3, 0, 1, 4)).reshape(3 * channels, 9 * channels)
     bias = jnp.broadcast_to(conv_bias[:, None], (channels, depth))
     out = convolve_smooth(rect, weights, bias, smooth_coef, views, bricks)

time: 113 us -> 105 us (0.929)
  waiting for transfers between devices: 46.4 us -> 0 us
  Pallas kernels: 48 us -> 93 us
  starting transfers between devices: 5.99 us -> 0 us
  other arithmetic: 2.49 us -> 0 us
  local copies, waits for them, and re-layouts: 9.19 us -> 10.7 us
    all_to_all x1 -> x0, waiting for transfers between devices: 46.4 us -> none  [on_device(): lax.all_to_all(partial, ('views', 'bricks'), split_axis=0, concat_axis=0,...]
    pallas_call x2 -> x1, Pallas kernels: 11.8 us -> 57.7 us  [exchange(): pl.pallas_call(functools.partial(exchange_kernel, views, bricks), out_sha...]
    all_to_all x1 -> x0, starting transfers between devices: 5.99 us -> none  [on_device(): lax.all_to_all(partial, ('views', 'bricks'), split_axis=0, concat_axis=0,...]
    convert_element_type x1 -> x0, other arithmetic: 1.24 us -> none  [on_device(): got_ids = got[:, got.shape[1] - 8, 0].astype(jnp.int32)]
    select_n x1 -> x0, other arithmetic: 1.24 us -> none  [on_device(): ids = jnp.where(live, voxel_ids, blocks)]
  transfers between devices with their start and end apart: 1 -> 0, of which waited for: 1 -> 0; matrix products, arithmetic and copies ran while one was open for 1% -> 0% of each run, Pallas kernels for 0% -> 0%
where the time goes in v1:
time: 105 us; the launch traced here: 104 us
  Pallas kernels  93 us (89%)
  local copies, waits for them, and re-layouts  10.7 us (10%)
    pallas_call x1, Pallas kernels, exchange(): pl.pallas_call(functools.partial(exchange_kernel, views, bricks), out_sha...  57.7 us
    pallas_call x1, Pallas kernels, convolve_smooth(): pl.pallas_call(functools.partial(conv_kernel, views, bricks), out_shape=j...  35.3 us
    transpose x1, local copies, waits for them, and re-layouts, on_device(): return jnp.transpose(out, (2, 0, 1, 3))  6.9 us

profile of v1, /device:TPU:12, one launch (start us, length us, event | category | flops | bytes accessed | tf_op | source)
XLA Modules:
  0.0 104.4 jit_solution(1350308790264064086)
XLA Ops:
  0.7 1.3 %broadcast_in_dim.2.bias_ref = f32[64,128]{1,0:T(8,128)} broadcast(f32[64]{0:T(128)} %param.14), dimensions={0} | broadcast | bytes 33024 | tf_op jit(solution)/shard_map/broadcast_in_dim | solution.py:443
  2.0 1.4 %copy.11 = bf16[3,64,3,3,64]{4,3,2,1,0:T(4,128)(2,1)S(1)} copy(bf16[3,64,3,3,64]{4,1,0,3,2:T(8,128)(2,1)} %bitcast.6) | data formatting | bytes 442368 | tf_op jit(solution)/shard_map/transpose | solution.py:442
  3.4 1.1 %reshape.4.w_ref = bf16[192,576]{1,0:T(8,128)(2,1)} reshape(bf16[3,64,3,3,64]{4,3,2,1,0:T(4,128)(2,1)S(1)} %copy.11) | data formatting | bytes 442368 | tf_op jit(solution)/shard_map/reshape | solution.py:442
  4.5 57.7 %exchange.1.r_ref = bf16[8,32,64,128]{3,2,1,0:T(8,128)(2,1)} custom-call(s32[1,1,32]{2,1,0:T(1,128)} %pixel_ref.1, s32[1,1,32]{2,1,0:T(1,128)} %voxel_ref.1, s32[1,1]{1,0:T(1,128)S(6)} %copy.13.count_ref, bf16[16,64,128]{2,1,0:T(8,128)(2,1)} %bitcast.7, bf16[32,128,512]{2,1,0:T(8,128)(2,1)} %bitcast.5), custom_call_target="tpu_custom_call" | custom-call | tf_op jit(solution)/shard_map/exchange/pallas_call | solution.py:182
  62.2 35.3 %conv.1 = bf16[8,32,64,128]{3,2,1,0:T(8,128)(2,1)} custom-call(bf16[8,32,64,128]{3,2,1,0:T(8,128)(2,1)} %exchange.1.r_ref, bf16[192,576]{1,0:T(8,128)(2,1)} %reshape.4.w_ref, f32[64,128]{1,0:T(8,128)} %broadcast_in_dim.2.bias_ref, f32[8,32,128]{2,1,0:T(8,128)} %coef_ref.1), custom_call_target="tpu_custom_call" | custom-call | tf_op jit(solution)/shard_map/conv/pallas_call | solution.py:409
  97.5 6.9 %copy.12 = bf16[64,8,32,128]{3,2,1,0:T(8,128)(2,1)} copy(bf16[64,8,32,128]{3,0,2,1:T(8,128)(2,1)} %bitcast.4) | data formatting | bytes 8388608 | tf_op jit(solution)/shard_map/transpose | solution.py:445

commit v2 on v1

v2 whole, which is shorter than its diff:
```python
import functools

import jax
import jax.numpy as jnp
from jax import lax
from jax.experimental import pallas as pl
from jax.experimental.pallas import tpu as pltpu
from jax.sharding import PartitionSpec as P

MESH = pl.DeviceIdType.MESH
GROUP = 4
RING = 32
LIMIT = 60 * 1024 * 1024
PAIRS = ((0, 1), (1, 2), (0, 2))


def lift_conv_kernel(
    views, bricks, pixel_ref, voxel_ref, count_ref, feats_ref, tiles_ref, w_ref, bias_ref,
    coef_ref, out_ref,
    tiles, part, got, sums, mark, marks, table, index, pad, acc, prod, obuf, pair, one, shift,
    tile_sem, send_sem, recv_sem, mark_send, mark_recv, table_sem, halo_send, halo_recv, out_sem,
):
    v = lax.axis_index("views")
    b = lax.axis_index("bricks")
    slots = voxel_ref.shape[2]
    ring = tiles.shape[0]
    me = v * bricks + b
    parts, _, ch, depth = part.shape
    size_x, size_y = obuf.shape[:2]
    across = size_y // parts
    blocks = size_x * across
    order = [parts - 1] + list(range(parts - 1))
    wide = 3 * ch

    def loop(low, high, body, unroll=1):
        def step(i, _):
            body(i)
            return 0

        lax.fori_loop(low, high, step, 0, unroll=unroll)

    def peer(k):
        turn = k + (views // 2) * bricks
        return lax.rem(v + turn // bricks, views), lax.rem(b + lax.rem(turn, bricks), bricks)

    def place(k):
        pv, pb = peer(k)
        return pv * bricks + pb

    own = (views - views // 2) * bricks % slots

    def fetch(k):
        slot = lax.rem(k, ring)
        return pltpu.make_async_copy(tiles_ref.at[place(k)], tiles.at[slot], tile_sem.at[slot])

    loop(0, ring, lambda k: fetch(k).start())
    barrier = pltpu.get_barrier_semaphore()

    def greet(k):
        @pl.when(k != own)
        def _():
            pl.semaphore_signal(barrier, inc=1, device_id=peer(k), device_id_type=MESH)

    loop(0, slots, greet)
    offset = lax.rem(me * 37, slots)

    def note(s):
        turn = lax.rem(s - offset + slots, slots)
        ident = jnp.where(turn < count_ref[0, 0], voxel_ref[0, 0, s], blocks)
        mark[s] = jnp.full(mark.shape[1:], ident, jnp.int32)

    loop(0, slots, note)

    def push(q, k):
        @pl.when(k != own)
        def _():
            pltpu.make_async_remote_copy(
                src_ref=part.at[q, place(k)], dst_ref=got.at[q, me],
                send_sem=send_sem.at[q], recv_sem=recv_sem.at[q],
                device_id=peer(k), device_id_type=MESH,
            ).start()

        @pl.when(k == own)
        def _():
            pltpu.make_async_copy(part.at[q, me], got.at[q, me], recv_sem.at[q]).start()

    def push_mark(k):
        @pl.when(k != own)
        def _():
            pltpu.make_async_remote_copy(
                src_ref=mark.at[place(k)], dst_ref=marks.at[me],
                send_sem=mark_send, recv_sem=mark_recv,
                device_id=peer(k), device_id_type=MESH,
            ).start()

        @pl.when(k == own)
        def _():
            pltpu.make_async_copy(mark.at[me], marks.at[me], mark_recv).start()

    def lift(k):
        slot = place(k)
        fetch(k).wait()
        value = jnp.dot(
            feats_ref[pixel_ref[0, 0, slot]], tiles[lax.rem(k, ring)],
            preferred_element_type=jnp.float32,
        ).astype(jnp.bfloat16)
        for q in range(parts):
            part[q, slot] = value[:, q * depth : (q + 1) * depth]
        if ring < slots:

            @pl.when(k + ring < slots)
            def _():
                fetch(k + ring).start()

    def lift_push(k):
        lift(k)
        push(order[0], k - 1)

    lift(0)
    pl.semaphore_wait(barrier, slots - 1)
    loop(1, slots, lift_push)
    push(order[0], slots - 1)
    loop(0, slots, push_mark)
    for q in order[1:]:
        loop(0, slots, lambda k, q=q: push(q, k))

    def there(dv, db):
        return (v + dv >= 0) & (v + dv < views) & (b + db >= 0) & (b + db < bricks)

    def low_row(q):
        return 1 if 2 * q >= parts else 0

    def edges(q):
        dv = 1 if 2 * q >= parts else -1
        return ((0, 1), (0, -1), (dv, 0), (dv, 1), (dv, -1))

    def span(q, dv, db):
        width = 2 if dv == 0 or q in (0, parts - 1) else 1
        if db == 0:
            from_x, to_x = pl.ds(2, size_x), pl.ds(2, size_x)
        elif db == 1:
            from_x, to_x = pl.ds(size_x + 2 - width, width), pl.ds(2 - width, width)
        else:
            from_x, to_x = pl.ds(2, width), pl.ds(size_x + 2, width)
        if dv == 0:
            return from_x, pl.ds(low_row(q), across), to_x, pl.ds(low_row(q), across)
        if dv == 1:
            return from_x, pl.ds(across, 1), to_x, pl.ds(0, 1)
        return from_x, pl.ds(0, 1), to_x, pl.ds(across, 1)

    def halo(q, k):
        dv, db = edges(q)[k]
        from_x, from_y, to_x, to_y = span(q, dv, db)
        return pltpu.make_async_remote_copy(
            src_ref=pad.at[q, from_x, from_y], dst_ref=pad.at[q, to_x, to_y],
            send_sem=halo_send.at[q, k], recv_sem=halo_recv.at[q, k],
            device_id=(v + dv, b + db), device_id_type=MESH,
        )

    for q in range(parts):
        for k, (dv, db) in enumerate(edges(q)):

            @pl.when(jnp.logical_not(there(-dv, -db)))
            def _(q=q, dv=dv, db=db):
                _, _, to_x, to_y = span(q, dv, db)
                view = pad.at[q, to_x, to_y]
                view[...] = jnp.zeros(view.shape, jnp.bfloat16)

    for dy in range(3):
        one[dy] = jnp.concatenate(
            [
                jnp.concatenate([w_ref[dx, dy, dz] for dz in range(3)], axis=0)
                for dx in range(3)
            ],
            axis=1,
        )
    for i, (first, second) in enumerate(PAIRS):
        pair[i] = jnp.concatenate([one[first], one[second]], axis=1)
    tall = lax.broadcasted_iota(jnp.int32, (ch, ch), 0)
    flat = lax.broadcasted_iota(jnp.int32, (ch, ch), 1)
    spread = jnp.where(tall == flat, jnp.broadcast_to(bias_ref[...], (ch, ch)), 0.0)
    shift[...] = jnp.broadcast_to(jnp.sum(spread, axis=1, keepdims=True), shift.shape)

    pltpu.make_async_copy(marks, marks, mark_recv).wait()
    lane = lax.broadcasted_iota(jnp.int32, marks.shape[1:], 1)
    row = jnp.full(lane.shape, -1, jnp.int32)
    row = lax.fori_loop(0, slots, lambda d, r: jnp.where(lane == d, marks[d], r), row)

    def newest(match):
        found = jnp.max(jnp.where(match, lane, -1), axis=1, keepdims=True)
        return jnp.where(found < 0, slots, found)

    table[0] = lax.fori_loop(
        0, slots,
        lambda d, t: jnp.where(lane == d, newest((row == marks[d]) & (lane < d)), t),
        jnp.zeros(lane.shape, jnp.int32),
    )
    table[1] = lax.fori_loop(
        0, blocks,
        lambda i, t: jnp.where(lane == i, newest(row == i), t),
        jnp.zeros(lane.shape, jnp.int32),
    )
    to_scalar = pltpu.make_async_copy(table, index, table_sem)
    to_scalar.start()
    to_scalar.wait()
    sums[slots] = jnp.zeros(sums.shape[1:], jnp.float32)

    def receive(q):
        pltpu.make_async_copy(got.at[q], got.at[q], recv_sem.at[q]).wait()

        def add(d):
            sums[d] = sums[index[0, 0, d]] + got[q, d].astype(jnp.float32)

        def put(i):
            i = lax.rem(i + (size_x - 2) * across, blocks)
            value = jnp.maximum(sums[index[1, 0, i]], 0.0).astype(jnp.bfloat16)
            pad[q, 2 + i // across, lax.rem(i, across) + low_row(q)] = value

        loop(0, slots, add, 4)
        loop(0, blocks, put, 4)
        for k, (dv, db) in enumerate(edges(q)):

            @pl.when(there(dv, db))
            def _(k=k):
                halo(q, k).start()

    def halos(q):
        for k, (dv, db) in enumerate(edges(q)):

            @pl.when(there(-dv, -db))
            def _(k=k):
                halo(q, k).wait_recv()

    wave = lax.broadcasted_iota(jnp.int32, (ch, depth), 1)

    def beside_z(low, high):
        before = jnp.where(wave == 0, 0.0, pltpu.roll(low, 1, 1))
        after = jnp.where(wave == depth - 1, 0.0, pltpu.roll(high, depth - 1, 1))
        return before + after

    def start(slot, job):
        items, q, sources, weight, first, final = job
        n = len(items) * depth
        tall = [
            jnp.concatenate([pad[p, g + dx, y + dy] for g, y in items], axis=1)
            for p, dy in sources
            for dx in range(3)
        ]
        prod[slot, :, 0:n] = jnp.dot(
            weight[...], jnp.concatenate(tall, axis=0), preferred_element_type=jnp.float32
        )

    def finish(slot, job, keep=None):
        items, q, sources, weight, first, final = job
        for j, (g, y) in enumerate(items):
            at = slice(j * depth, (j + 1) * depth)
            value = prod[slot, ch : 2 * ch, at]
            value = value + beside_z(prod[slot, 0:ch, at], prod[slot, 2 * ch : wide, at])
            if not first:
                value = value + acc[g, q, y]
            if final:
                value = jnp.maximum(value + shift[...], 0.0)
                if keep is not None:
                    value = value * keep
            acc[g, q, y] = value

    def place_of(y):
        q = y % parts
        return q, y // parts + low_row(q)

    def smooth(x, y):
        here = acc[(x + 1,) + place_of(y)]
        beside = acc[(x,) + place_of(y)] + acc[(x + 2,) + place_of(y)]
        beside = beside + acc[(x + 1,) + place_of(y - 1)] + acc[(x + 1,) + place_of(y + 1)]
        beside = beside + beside_z(here, here)
        coef = coef_ref[x, y : y + 1, :]
        obuf[x, y] = (here + coef * (beside - 6.0 * here)).astype(jnp.bfloat16)

    def put_out(x):
        pltpu.make_async_copy(obuf.at[x], out_ref.at[x], out_sem.at[x]).start()

    def run(jobs, x=None, rows=(), keep=None):
        each = -(-len(rows) // len(jobs))
        for i, job in enumerate(jobs):
            start(i % 2, job)
            for y in rows[i * each : (i + 1) * each]:
                smooth(x, y)
            if i:
                finish((i - 1) % 2, jobs[i - 1], keep)
        finish((len(jobs) - 1) % 2, jobs[-1], keep)

    def plane(g, q, sources, weight, first, final):
        low = low_row(q)
        ys = [low + i for i in range(across)]
        return [
            ([(g, y) for y in ys[i : i + GROUP]], q, sources, weight, first, final)
            for i in range(0, across, GROUP)
        ]

    def line(y, q, sources, weight, first, final):
        gs = [1 + i for i in range(size_x)]
        return [
            ([(g, y) for g in gs[i : i + GROUP]], q, sources, weight, first, final)
            for i in range(0, size_x, GROUP)
        ]

    last = parts - 1
    both = ((last, 0), (0, 0))

    def wipe(gs, qs, ys):
        for g in gs:
            for q in qs:
                for y in ys:
                    acc[g, q, y] = jnp.zeros((ch, depth), jnp.float32)

    receive(order[0])
    receive(order[1])
    halos(order[0])
    halos(order[1])
    loop(
        0, size_x + 2,
        lambda g: run(
            plane(g, 0, both, pair.at[0], True, False)
            + plane(g, last, both, pair.at[1], True, False)
        ),
    )
    run(
        line(across, 0, both, pair.at[0], True, False)
        + line(0, last, both, pair.at[1], True, False)
    )
    receive(order[2])
    halos(order[2])
    loop(
        0, size_x + 2,
        lambda g: run(
            plane(g, 0, ((1, 0),), one.at[2], False, True)
            + plane(g, 1, ((0, 0), (1, 0)), pair.at[0], True, False)
            + plane(g, 2, ((1, -1), (last, 0)), pair.at[2], True, False)
        ),
    )
    run(line(across, 0, ((1, 0),), one.at[2], False, True))

    @pl.when(v == views - 1)
    def _():
        wipe(range(1, size_x + 1), (0,), (across,))

    @pl.when(b == 0)
    def _():
        wipe((0,), (0,), range(across))

    @pl.when(b == bricks - 1)
    def _():
        wipe((size_x + 1,), (0,), range(across))

    receive(order[3])

    def close(g):
        return (
            plane(g, 1, ((2, 1),), one.at[2], False, True)
            + plane(g, 2, ((2, 0),), one.at[1], False, True)
            + plane(g, last, ((2, 0),), one.at[0], False, True)
        )

    inner = list(range(1, size_y))
    whole = list(range(size_y))
    loop(2, 5, lambda g: run(close(g)))
    loop(5, size_x, lambda g: run(close(g), g - 3, inner))
    halos(order[3])
    run(line(0, last, ((2, 0),), one.at[0], False, True))

    @pl.when(v == 0)
    def _():
        wipe(range(1, size_x + 1), (last,), (0,))

    def early(x):
        smooth(x, 0)
        put_out(x)

    loop(2, size_x - 3, early)

    def rest(i):
        low = lax.rem(i, 2) == 0
        g = jnp.where(low, 1 - i // 2, size_x + i // 2)
        x = jnp.where(
            i == 0, size_x - 3, jnp.where(i == 1, 1, jnp.where(i == 2, size_x - 2, 0))
        )
        fits = jnp.where(i < 2, 0, jnp.where(low, b, bricks - 1 - b) - 1) >= 0
        run(close(g), x, whole, jnp.where(fits, 1.0, 0.0))
        put_out(x)

    loop(0, 4, rest)

    def ending(i):
        for j in range(parts):
            smooth_last(i, j)

    def smooth_last(k, q):
        x = size_x - 1
        base = k + low_row(q)

        def spot(p):
            if p < 0:
                return parts - 1, k + low_row(parts - 1) - 1
            if p >= parts:
                return 0, k + 1 + low_row(0)
            return p, k + low_row(p)

        here = acc[x + 1, q, base]
        beside = acc[x, q, base] + acc[x + 2, q, base]
        beside = beside + acc[(x + 1,) + spot(q - 1)] + acc[(x + 1,) + spot(q + 1)]
        beside = beside + beside_z(here, here)
        coef = coef_ref[x, pl.ds(k * parts + q, 1), :]
        value = here + coef * (beside - 6.0 * here)
        obuf[x, k * parts + q] = value.astype(jnp.bfloat16)

    loop(0, across, ending)
    put_out(size_x - 1)
    for x in range(size_x):
        pltpu.make_async_copy(obuf.at[x], out_ref.at[x], out_sem.at[x]).wait()
    for q in range(parts):
        sent = part.at[q, pl.ds(0, slots - 1)]
        pltpu.make_async_copy(sent, sent, send_sem.at[q]).wait()
        for k, (dv, db) in enumerate(edges(q)):

            @pl.when(there(dv, db))
            def _(q=q, k=k):
                halo(q, k).wait_send()

    sent = mark.at[pl.ds(0, slots - 1)]
    pltpu.make_async_copy(sent, sent, mark_send).wait()


def lift_conv(pixel, voxel, count, feats, tiles, weight, bias, coef, views, bricks):
    slots, pixels, voxels = tiles.shape
    ch = feats.shape[1]
    size_x, size_y, depth = coef.shape
    parts = voxels // depth
    across = size_y // parts
    assert parts == 4
    smem = pl.BlockSpec(memory_space=pltpu.SMEM)
    vmem = pl.BlockSpec(memory_space=pltpu.VMEM)
    anyspec = pl.BlockSpec(memory_space=pl.ANY)
    dma = pltpu.SemaphoreType.DMA
    return pl.pallas_call(
        functools.partial(lift_conv_kernel, views, bricks),
        out_shape=jax.ShapeDtypeStruct((size_x, size_y, ch, depth), jnp.bfloat16),
        in_specs=[smem, smem, smem, vmem, anyspec, vmem, vmem, vmem],
        out_specs=anyspec,
        scratch_shapes=[
            pltpu.VMEM((min(slots, RING), pixels, voxels), jnp.bfloat16),
            pltpu.VMEM((parts, slots, ch, depth), jnp.bfloat16),
            pltpu.VMEM((parts, slots, ch, depth), jnp.bfloat16),
            pltpu.VMEM((slots + 1, ch, depth), jnp.float32),
            pltpu.VMEM((slots, 8, 128), jnp.int32),
            pltpu.VMEM((slots, 8, 128), jnp.int32),
            pltpu.VMEM((2, 8, 128), jnp.int32),
            pltpu.SMEM((2, 8, 128), jnp.int32),
            pltpu.VMEM((parts, size_x + 4, across + 1, ch, depth), jnp.bfloat16),
            pltpu.VMEM((size_x + 2, parts, across + 1, ch, depth), jnp.float32),
            pltpu.VMEM((2, 3 * ch, GROUP * depth), jnp.float32),
            pltpu.VMEM((size_x, size_y, ch, depth), jnp.bfloat16),
            pltpu.VMEM((3, 3 * ch, 6 * ch), jnp.bfloat16),
            pltpu.VMEM((3, 3 * ch, 3 * ch), jnp.bfloat16),
            pltpu.VMEM((ch, depth), jnp.float32),
            dma((min(slots, RING),)),
            dma((parts,)),
            dma((parts,)),
            dma,
            dma,
            dma,
            dma((parts, 5)),
            dma((parts, 5)),
            dma((size_x,)),
        ],
        compiler_params=pltpu.CompilerParams(
            collective_id=0, has_side_effects=True, vmem_limit_bytes=LIMIT
        ),
        name="lift_conv",
    )(pixel, voxel, count, feats, tiles, weight, bias, coef)


def turn_kernel(in_ref, out_ref, stage):
    size_y, ch, depth = in_ref.shape[1:]
    for y in range(size_y):
        stage[pl.ds(y, ch, stride=size_y), :] = in_ref[0, y].astype(jnp.float32)
    out_ref[...] = stage[...].reshape(ch, 1, size_y, depth).astype(jnp.bfloat16)


def turn(x):
    size_x, size_y, ch, depth = x.shape
    return pl.pallas_call(
        turn_kernel,
        out_shape=jax.ShapeDtypeStruct((ch, size_x, size_y, depth), jnp.bfloat16),
        grid=(size_x,),
        in_specs=[pl.BlockSpec((1, size_y, ch, depth), lambda i: (i, 0, 0, 0))],
        out_specs=pl.BlockSpec((ch, 1, size_y, depth), lambda i: (0, i, 0, 0)),
        scratch_shapes=[pltpu.VMEM((ch * size_y, depth), jnp.float32)],
        name="turn",
    )(x)


def on_device(
    views, bricks,
    tile_pixel, tile_voxel, tile_count, features, interp, conv_weight, conv_bias, smooth_coef
):
    out = lift_conv(
        tile_pixel, tile_voxel, tile_count, features[0, 0], interp[0, 0],
        conv_weight, conv_bias[None], smooth_coef, views, bricks,
    )
    return turn(out)


def solution(mesh):
    in_specs = (
        P("views", "bricks", None),
        P("views", "bricks", None),
        P("views", "bricks"),
        P("views", "bricks", None, None, None),
        P("views", "bricks", None, None, None),
        P(),
        P(),
        P("bricks", "views", None),
    )
    out_specs = P(None, "bricks", "views", None)
    body = functools.partial(on_device, mesh.shape["views"], mesh.shape["bricks"])
    return jax.shard_map(body, mesh=mesh, in_specs=in_specs, out_specs=out_specs, check_vma=False)
```

time: 105 us -> 116 us (1.10)
  Pallas kernels: 93 us -> 115 us
  local copies, waits for them, and re-layouts: 10.7 us -> 0 us
    pallas_call x2, Pallas kernels: 93 us -> 115 us  [the longest x1 103 us: lift_conv(): pl.pallas_call(functools.partial(lift_conv_kernel, views, bricks), out_sh...]
    transpose x2 -> x0, local copies, waits for them, and re-layouts: 8.3 us -> none  [the longest x1 6.9 us: on_device(): return jnp.transpose(out, (2, 0, 1, 3))]
    broadcast_in_dim x1 -> x0, local copies, waits for them, and re-layouts: 1.33 us -> none  [on_device(): bias = jnp.broadcast_to(conv_bias[:, None], (channels, depth))]
where the time goes in v2:
time: 116 us; the launch traced here: 115 us
  Pallas kernels  115 us (99%)
    pallas_call x1, Pallas kernels, lift_conv(): pl.pallas_call(functools.partial(lift_conv_kernel, views, bricks), out_sh...  103 us
    pallas_call x1, Pallas kernels, turn(): pl.pallas_call(turn_kernel, out_shape=jax.ShapeDtypeStruct((ch, size_x, s...  11.1 us

profile of v2, /device:TPU:12, one launch (start us, length us, event | category | flops | bytes accessed | tf_op | source)
XLA Modules:
  0.0 115.2 jit_solution(16833480335648940103)
XLA Ops:
  0.7 103.5 %lift_conv.1.in_ref = bf16[8,32,64,128]{3,2,1,0:T(8,128)(2,1)} custom-call(s32[1,1,32]{2,1,0:T(1,128)} %pixel_ref.1, s32[1,1,32]{2,1,0:T(1,128)} %voxel_ref.1, s32[1,1]{1,0:T(1,128)S(6)} %copy.9.count_ref, bf16[16,64,128]{2,1,0:T(8,128)(2,1)} %bitcast.4, bf16[32,128,512]{2,1,0:T(8,128)(2,1)} %bitcast.3, bf16[3,3,3,64,64]{4,3,2,1,0:T(8,128)(2,1)} %w_ref.1, ...), custom_call_target="tpu_custom_call" | custom-call | tf_op jit(solution)/shard_map/lift_conv/pallas_call | solution.py:444
  104.1 11.1 %turn.1 = bf16[64,8,32,128]{3,2,1,0:T(8,128)(2,1)} custom-call(bf16[8,32,64,128]{3,2,1,0:T(8,128)(2,1)} %lift_conv.1.in_ref), custom_call_target="tpu_custom_call" | custom-call | tf_op jit(solution)/shard_map/turn/pallas_call | solution.py:491

commit v3 on v2

--- a/solution.py
+++ b/solution.py
@@ -17,7 +17,7 @@
 def lift_conv_kernel(
     views, bricks, pixel_ref, voxel_ref, count_ref, feats_ref, tiles_ref, w_ref, bias_ref,
     coef_ref, out_ref,
-    tiles, part, got, sums, mark, marks, table, index, pad, acc, prod, obuf, pair, one, shift,
+    tiles, part, got, sums, mark, marks, table, index, pad, acc, prod, obuf, pair, one, full, shift,
     tile_sem, send_sem, recv_sem, mark_send, mark_recv, table_sem, halo_send, halo_recv, out_sem,
 ):
     v = lax.axis_index("views")
@@ -176,6 +176,7 @@
         )
     for i, (first, second) in enumerate(PAIRS):
         pair[i] = jnp.concatenate([one[first], one[second]], axis=1)
+    full[...] = jnp.concatenate([one[dy] for dy in range(3)], axis=1)
     tall = lax.broadcasted_iota(jnp.int32, (ch, ch), 0)
     flat = lax.broadcasted_iota(jnp.int32, (ch, ch), 1)
     spread = jnp.where(tall == flat, jnp.broadcast_to(bias_ref[...], (ch, ch)), 0.0)
@@ -290,18 +291,20 @@
         finish((len(jobs) - 1) % 2, jobs[-1], keep)
 
     def plane(g, q, sources, weight, first, final):
-        low = low_row(q)
-        ys = [low + i for i in range(across)]
+        low = 0 if q == 1 else 1
+        high = across + 1 if q == 2 else across
+        ys = list(range(low, high))
         return [
             ([(g, y) for y in ys[i : i + GROUP]], q, sources, weight, first, final)
-            for i in range(0, across, GROUP)
+            for i in range(0, len(ys), GROUP)
         ]
 
-    def line(y, q, sources, weight, first, final):
-        gs = [1 + i for i in range(size_x)]
+    def line(y, q, gs):
+        before, after = (q - 1) % parts, (q + 1) % parts
+        sources = ((before, 0), (q, 0), (after, 0))
         return [
-            ([(g, y) for g in gs[i : i + GROUP]], q, sources, weight, first, final)
-            for i in range(0, size_x, GROUP)
+            ([(g, y) for g in gs[i : i + GROUP]], q, sources, full, True, True)
+            for i in range(0, len(gs), GROUP)
         ]
 
     last = parts - 1
@@ -313,45 +316,27 @@
                 for y in ys:
                     acc[g, q, y] = jnp.zeros((ch, depth), jnp.float32)
 
-    receive(order[0])
-    receive(order[1])
-    halos(order[0])
-    halos(order[1])
-    loop(
-        0, size_x + 2,
-        lambda g: run(
+    def first_pass(g):
+        run(
             plane(g, 0, both, pair.at[0], True, False)
             + plane(g, last, both, pair.at[1], True, False)
-        ),
-    )
-    run(
-        line(across, 0, both, pair.at[0], True, False)
-        + line(0, last, both, pair.at[1], True, False)
-    )
-    receive(order[2])
-    halos(order[2])
-    loop(
-        0, size_x + 2,
-        lambda g: run(
+        )
+
+    def second_pass(g):
+        run(
             plane(g, 0, ((1, 0),), one.at[2], False, True)
             + plane(g, 1, ((0, 0), (1, 0)), pair.at[0], True, False)
             + plane(g, 2, ((1, -1), (last, 0)), pair.at[2], True, False)
-        ),
-    )
-    run(line(across, 0, ((1, 0),), one.at[2], False, True))
-
-    @pl.when(v == views - 1)
-    def _():
-        wipe(range(1, size_x + 1), (0,), (across,))
-
-    @pl.when(b == 0)
-    def _():
-        wipe((0,), (0,), range(across))
-
-    @pl.when(b == bricks - 1)
-    def _():
-        wipe((size_x + 1,), (0,), range(across))
-
+        )
+
+    def outer(i):
+        return jnp.where(i < 2, i, size_x - 2 + i)
+
+    receive(order[0])
+    receive(order[1])
+    loop(2, size_x, first_pass)
+    receive(order[2])
+    loop(2, size_x, second_pass)
     receive(order[3])
 
     def close(g):
@@ -361,19 +346,37 @@
             + plane(g, last, ((2, 0),), one.at[0], False, True)
         )
 
-    inner = list(range(1, size_y))
+    inner = list(range(2, size_y - 2))
     whole = list(range(size_y))
     loop(2, 5, lambda g: run(close(g)))
     loop(5, size_x, lambda g: run(close(g), g - 3, inner))
+    halos(order[0])
+    halos(order[1])
+    loop(0, 4, lambda i: first_pass(outer(i)))
+    halos(order[2])
+    loop(0, 4, lambda i: second_pass(outer(i)))
     halos(order[3])
-    run(line(0, last, ((2, 0),), one.at[0], False, True))
+    near, far = list(range(1, size_x + 1)), list(range(size_x + 2))
+    run(line(0, last, near) + line(across, 0, near) + line(0, 0, far) + line(across, last, far))
 
     @pl.when(v == 0)
     def _():
-        wipe(range(1, size_x + 1), (last,), (0,))
+        wipe(near, (last,), (0,))
+
+    @pl.when(v == views - 1)
+    def _():
+        wipe(near, (0,), (across,))
+
+    for g, edge in ((0, b == 0), (size_x + 1, b == bricks - 1)):
+
+        @pl.when(edge)
+        def _(g=g):
+            wipe((g,), (0,), range(across))
+            wipe((g,), (last,), (across,))
 
     def early(x):
-        smooth(x, 0)
+        for y in (0, 1, size_y - 2, size_y - 1):
+            smooth(x, y)
         put_out(x)
 
     loop(2, size_x - 3, early)
@@ -461,6 +464,7 @@
             pltpu.VMEM((size_x, size_y, ch, depth), jnp.bfloat16),
             pltpu.VMEM((3, 3 * ch, 6 * ch), jnp.bfloat16),
             pltpu.VMEM((3, 3 * ch, 3 * ch), jnp.bfloat16),
+            pltpu.VMEM((3 * ch, 9 * ch), jnp.bfloat16),
             pltpu.VMEM((ch, depth), jnp.float32),
             dma((min(slots, RING),)),
             dma((parts,)),
@@ -479,26 +483,6 @@
     )(pixel, voxel, count, feats, tiles, weight, bias, coef)
 
 
-def turn_kernel(in_ref, out_ref, stage):
-    size_y, ch, depth = in_ref.shape[1:]
-    for y in range(size_y):
-        stage[pl.ds(y, ch, stride=size_y), :] = in_ref[0, y].astype(jnp.float32)
-    out_ref[...] = stage[...].reshape(ch, 1, size_y, depth).astype(jnp.bfloat16)
-
-
-def turn(x):
-    size_x, size_y, ch, depth = x.shape
-    return pl.pallas_call(
-        turn_kernel,
-        out_shape=jax.ShapeDtypeStruct((ch, size_x, size_y, depth), jnp.bfloat16),
-        grid=(size_x,),
-        in_specs=[pl.BlockSpec((1, size_y, ch, depth), lambda i: (i, 0, 0, 0))],
-        out_specs=pl.BlockSpec((ch, 1, size_y, depth), lambda i: (0, i, 0, 0)),
-        scratch_shapes=[pltpu.VMEM((ch * size_y, depth), jnp.float32)],
-        name="turn",
-    )(x)
-
-
 def on_device(
     views, bricks,
     tile_pixel, tile_voxel, tile_count, features, interp, conv_weight, conv_bias, smooth_coef
@@ -507,7 +491,7 @@
         tile_pixel, tile_voxel, tile_count, features[0, 0], interp[0, 0],
         conv_weight, conv_bias[None], smooth_coef, views, bricks,
     )
-    return turn(out)
+    return jnp.transpose(out, (2, 0, 1, 3))
 
 
 def solution(mesh):

time: 116 us -> 94.1 us (0.81)
  Pallas kernels: 115 us -> 86 us
  local copies, waits for them, and re-layouts: 0 us -> 6.9 us
    pallas_call x1, Pallas kernels: 103 us -> 86 us  [lift_conv(): pl.pallas_call(functools.partial(lift_conv_kernel, views, bricks), out_sh...]
    pallas_call x1 -> x0, Pallas kernels: 11.1 us -> none  [turn(): pl.pallas_call(turn_kernel, out_shape=jax.ShapeDtypeStruct((ch, size_x, s...]
    transpose x0 -> x1, local copies, waits for them, and re-layouts: none -> 6.9 us  [on_device(): return jnp.transpose(out, (2, 0, 1, 3))]
where the time goes in v3:
time: 94.1 us; the launch traced here: 93.5 us
  Pallas kernels  86 us (91%)
  local copies, waits for them, and re-layouts  6.9 us (7%)
    pallas_call x1, Pallas kernels, lift_conv(): pl.pallas_call(functools.partial(lift_conv_kernel, views, bricks), out_sh...  86 us
    transpose x1, local copies, waits for them, and re-layouts, on_device(): return jnp.transpose(out, (2, 0, 1, 3))  6.9 us

profile of v3, /device:TPU:12, one launch (start us, length us, event | category | flops | bytes accessed | tf_op | source)
XLA Modules:
  0.0 93.5 jit_solution(12206843650598861019)
XLA Ops:
  0.7 86.0 %lift_conv.1 = bf16[8,32,64,128]{3,2,1,0:T(8,128)(2,1)} custom-call(s32[1,1,32]{2,1,0:T(1,128)} %pixel_ref.1, s32[1,1,32]{2,1,0:T(1,128)} %voxel_ref.1, s32[1,1]{1,0:T(1,128)S(6)} %copy.10.count_ref, bf16[16,64,128]{2,1,0:T(8,128)(2,1)} %bitcast.6, bf16[32,128,512]{2,1,0:T(8,128)(2,1)} %bitcast.5, bf16[3,3,3,64,64]{4,3,2,1,0:T(8,128)(2,1)} %w_ref.1, ...), custom_call_target="tpu_custom_call" | custom-call | tf_op jit(solution)/shard_map/lift_conv/pallas_call | solution.py:447
  86.6 6.9 %copy.9 = bf16[64,8,32,128]{3,2,1,0:T(8,128)(2,1)} copy(bf16[64,8,32,128]{3,0,2,1:T(8,128)(2,1)} %bitcast.4) | data formatting | bytes 8388608 | tf_op jit(solution)/shard_map/transpose | solution.py:494
